TPU v7x, 32 devices: a whole 2x2x4 slice. The times are simulated.
32 devices in a mesh: rows: 8 (over z, y), rep: 4 (over x, core).
Axes of the slice: x: 2, y: 2, z: 4, core: 2. Of those that a mesh axis runs over, the one named last changes fastest.
Arguments:
- embed: bfloat16 [4096, 1024], P('rows'), may hold values from -6 to 6
- start: bfloat16 [4096, 128], P('rows'), may hold values from -6 to 6
- links: int32 [8, 8], P('rows'), may hold values from -1 to 3, as said below
Outputs:
- embedding: float32 [4096, 128], P('rows')
Inputs may be any that keep to these rules, and one draw needn't show every extreme that they name: `links`: entry [r, s] is -1 (no pair) or a block of owner s; the diagonal is -1; each row has at most 6 entries other than -1, and some row has exactly 6.
All inputs are finite; a program needn't handle non-finite values.
Results may differ from a plain program's by a relative error of at most 0.012.
Values may be sent and summed in bfloat16 or wider, within the bound.
A program may use at most 128 MiB of HBM per device.

v0:
```python
import math
import jax
import jax.numpy as jnp
from jax import lax
from jax.sharding import PartitionSpec as P

BLOCK = 128
BLOCKS_DEV = 4
ITERS = 2
EPSILON = 1e-06


def row_scale(rows):
    values = rows.astype(jnp.float32)
    return lax.rsqrt(jnp.mean(values * values, axis=-1) + EPSILON)


def orthonormal(result, gram_matrix):
    lower_factor = jnp.linalg.cholesky(gram_matrix)
    return lax.linalg.triangular_solve(
        lower_factor, result, left_side=False, lower=True, transpose_a=True
    )


def quarter_of(values, blocks, rep_count, quarter_index):
    shaped = values.reshape(
        (blocks, rep_count, values.shape[0] // (blocks * rep_count)) + values.shape[1:]
    )
    return lax.dynamic_index_in_dim(shaped, quarter_index, 1, keepdims=False)


def widen(block_part, rep_count, quarter_index):
    choose = (jnp.arange(rep_count) == quarter_index).astype(jnp.float32)
    expanded = block_part[:, None] * choose.reshape((1, rep_count) + (1,) * (block_part.ndim - 1))
    return expanded.reshape((-1,) + block_part.shape[2:])


def on_device(embed, start, links):
    rows_count = lax.axis_size("rows")
    rep_count = lax.axis_size("rep")
    quarter_index = lax.axis_index("rep")
    slab_rows, feature_count = embed.shape
    comp_count = start.shape[1]
    blocks = BLOCKS_DEV
    piece_rows = BLOCK // rep_count
    spread = 2.0 / math.sqrt(feature_count)
    highest = lax.Precision.HIGHEST
    slab_scale = row_scale(embed)
    own_quarter = quarter_of(embed, blocks, rep_count, quarter_index)
    quarter_scale = row_scale(own_quarter)
    link_row = links.reshape(rows_count)
    alive_dense = (link_row >= 0).astype(jnp.float32)
    asked_for = lax.all_to_all(
        links.reshape(rows_count, 1), "rows", split_axis=0, concat_axis=0, tiled=True
    )[:, 0]
    picked = jnp.clip(asked_for, 0, blocks - 1)
    placer = (asked_for[:, None] == jnp.arange(blocks)[None, :]).astype(jnp.float32)
    outgoing = jnp.take(own_quarter, picked, axis=0)
    pieces = lax.all_to_all(outgoing, "rows", split_axis=0, concat_axis=0, tiled=True)
    piece_scale = row_scale(pieces)
    products_in = jnp.einsum("pnd,rd->pnr", pieces, embed, preferred_element_type=jnp.float32)
    exponent = spread * products_in * piece_scale[:, :, None] * slab_scale[None, None, :]
    pair_tiles = (jnp.exp(exponent) * alive_dense[:, None, None]).astype(jnp.bfloat16)
    diag_products = jnp.einsum(
        "bnd,rd->bnr", own_quarter, embed, preferred_element_type=jnp.float32
    )
    diag_exponent = spread * diag_products * quarter_scale[:, :, None] * slab_scale[None, None, :]
    row_ids = (
        jnp.arange(blocks)[:, None] * BLOCK
        + quarter_index * piece_rows
        + jnp.arange(piece_rows)[None, :]
    )
    self_mask = row_ids[:, :, None] == jnp.arange(slab_rows)[None, None, :]
    diag_tile = (
        jnp.where(self_mask, 0.0, jnp.exp(diag_exponent))
        .astype(jnp.bfloat16)
        .reshape(blocks * piece_rows, slab_rows)
    )
    own_sums = jnp.sum(pair_tiles, axis=(0, 1), dtype=jnp.float32) + jnp.sum(
        diag_tile, axis=0, dtype=jnp.float32
    )
    back_sums = jnp.sum(pair_tiles, axis=2, dtype=jnp.float32)
    got_sums = lax.all_to_all(back_sums, "rows", split_axis=0, concat_axis=0, tiled=True)
    placed_sums = jnp.dot(placer.T, got_sums, precision=highest)
    degree = lax.psum(own_sums + widen(placed_sums, rep_count, quarter_index), "rep")
    inv_root = lax.rsqrt(degree)
    current = start.astype(jnp.float32)
    scaled = (current * inv_root[:, None]).astype(jnp.bfloat16)
    for turn_index in range(ITERS):
        scaled_quarter = quarter_of(scaled, blocks, rep_count, quarter_index)
        outgoing_iterate = jnp.take(scaled_quarter, picked, axis=0)
        reverse = jnp.einsum("pnr,rk->pnk", pair_tiles, scaled, preferred_element_type=jnp.float32)
        returned = lax.all_to_all(reverse, "rows", split_axis=0, concat_axis=0, tiled=True)
        fetched = lax.all_to_all(outgoing_iterate, "rows", split_axis=0, concat_axis=0, tiled=True)
        forward = lax.dot_general(
            pair_tiles, fetched, (((0, 1), (0, 1)), ((), ())), preferred_element_type=jnp.float32
        )
        forward = forward + lax.dot_general(
            diag_tile,
            scaled_quarter.reshape(blocks * piece_rows, comp_count),
            (((0,), (0,)), ((), ())),
            preferred_element_type=jnp.float32,
        )
        placed = jnp.einsum("pb,pnk->bnk", placer, returned, precision=highest)
        summed_part = forward + widen(placed, rep_count, quarter_index)
        summed_all = lax.psum(summed_part, "rep")
        result = summed_all * inv_root[:, None]
        gram_matrix = lax.psum(jnp.dot(result.T, result, precision=highest), "rows")
        current = orthonormal(result, gram_matrix)
        scaled = (current * inv_root[:, None]).astype(jnp.bfloat16)
    return current * math.sqrt(slab_rows * rows_count)


def solution(mesh):
    return jax.shard_map(
        on_device,
        mesh=mesh,
        in_specs=(P("rows", None), P("rows", None), P("rows", None)),
        out_specs=P("rows", None),
        check_vma=False,
    )
```

profile of v0, /device:TPU:0, one launch (start us, length us, event | category | flops | bytes accessed | tf_op | source)
XLA Modules:
  0.0 369.6 jit_solution(8929522240494461467)
XLA Ops:
  6.5 1.4 copy.25
  7.9 7.3 %all-to-all-start = ((s32[8,1,1]{2,1,0:T(1,128)}), s32[8,1,1]{2,1,0:T(1,128)S(1)}, u32[]{:S(2)}, u32[]{:S(2)}) async-start(s32[8,1,1]{2,1,0:T(1,128)} %copy.25), calls=%async_computation | async-start | bytes 8192 | tf_op jit(solution)/shard_map/all_to_all | solution.py:53
  15.3 1.5 multiply_reduce_fusion
  16.9 0.1 multiply_reduce_fusion.2
  17.1 0.1 mul.174
  17.2 4.5 %all-to-all-done = s32[8,1,1]{2,1,0:T(1,128)S(1)} async-done(((s32[8,1,1]{2,1,0:T(1,128)}), s32[8,1,1]{2,1,0:T(1,128)S(1)}, u32[]{:S(2)}, u32[]{:S(2)}) %all-to-all-start) | async-done | bytes 64 | tf_op jit(solution)/shard_map/all_to_all | solution.py:53
  21.7 0.4 fusion.50
  22.1 0.6 gather_fusion
  22.7 0.9 broadcast_select_fusion
  23.6 3.5 all-to-all-start.1
  27.1 0.5 convert_reduce_fusion.2
  27.7 12.7 %all-to-all-done.1 = bf16[8,32,1024]{2,1,0:T(8,128)(2,1)S(1)} async-done(((bf16[8,32,1024]{2,1,0:T(8,128)(2,1)}), bf16[8,32,1024]{2,1,0:T(8,128)(2,1)S(1)}, u32[]{:S(2)}, u32[]{:S(2)}) %all-to-all-start.1) | async-done | bytes 524320 | tf_op jit(solution)/shard_map/all_to_all | solution.py:59
  40.4 0.2 multiply_reduce_fusion.1
  40.6 1.2 convert_reduce_fusion.1
  41.8 3.7 all-to-all-start.2
  45.4 6.4 %all-to-all-done.2 = f32[8,1,32]{2,1,0:T(1,128)S(1)} async-done(((f32[8,1,32]{2,1,0:T(1,128)}), f32[8,1,32]{2,1,0:T(1,128)S(1)}, u32[]{:S(2)}, u32[]{:S(2)}) %all-to-all-start.2) | async-done | bytes 1056 | tf_op jit(solution)/shard_map/all_to_all | solution.py:83
  51.9 0.1 fusion.42
  52.0 0.1 mul.172
  52.1 5.7 %psum.35 = f32[512]{0:T(512)S(1)} all-reduce(f32[512]{0:T(512)S(1)} %multiply_add_fusion), channel_id=1, replica_groups=mesh['rows'=8,'rep'=4] {'rep'}, use_global_device_ids=true, to_apply=%region_6.7 | all-reduce | flops 512 | bytes 4096 | tf_op jit(solution)/shard_map/psum | solution.py:85
  57.7 0.1 multiply_convert_fusion
  57.9 0.6 gather_fusion.1
  58.5 0.7 broadcast_select_fusion.1
  59.2 3.3 all-to-all-start.3
  62.5 0.9 fusion.23
  63.4 6.0 %all-to-all-done.3 = bf16[8,32,128]{2,1,0:T(8,128)(2,1)S(1)} async-done(((bf16[8,32,128]{2,1,0:T(8,128)(2,1)}), bf16[8,32,128]{2,1,0:T(8,128)(2,1)S(1)}, u32[]{:S(2)}, u32[]{:S(2)}) %all-to-all-start.3) | async-done | bytes 65568 | tf_op jit(solution)/shard_map/all_to_all | solution.py:94
  69.4 3.4 all-to-all-start.4
  72.8 0.3 convolution_bitcast_fusion.3
  73.1 6.9 %all-to-all-done.4 = f32[8,32,128]{2,1,0:T(8,128)S(1)} async-done(((f32[8,32,128]{2,1,0:T(8,128)}), f32[8,32,128]{2,1,0:T(8,128)S(1)}, u32[]{:S(2)}, u32[]{:S(2)}) %all-to-all-start.4) | async-done | bytes 131104 | tf_op jit(solution)/shard_map/all_to_all | solution.py:93
  80.0 0.3 fusion.27
  80.3 0.1 bitcast_multiply_fusion.1
  80.4 0.9 fusion.5
  81.4 30.4 %all-reduce.5.cloned.1.call-done = f32[512,128]{1,0:T(8,128)} async-done(((f32[512,128]{1,0:T(8,128)}), f32[512,128]{1,0:T(8,128)}) %all-reduce.5.cloned.1.call-update) | async-done | bytes 262160 | tf_op jit(solution)/shard_map/psum | solution.py:106
  111.8 2.5 fusion.19
  114.3 70.2 %all-reduce.7.cloned.1.call-done = f32[128,128]{0,1:T(8,128)} async-done(((f32[128,128]{0,1:T(8,128)}), f32[128,128]{0,1:T(8,128)}) %all-reduce.7.cloned.1.call-update) | async-done | bytes 65552 | tf_op jit(solution)/shard_map/psum | solution.py:108
  184.5 0.9 copy.30
  185.4 0.9 fusion.38
  186.3 11.7 %cholesky.44 = f32[128,128]{1,0:T(8,128)S(1)} custom-call(f32[128,128]{1,0:T(8,128)S(1)} %fusion.38), custom_call_target="Cholesky" | custom-call | tf_op jit(solution)/shard_map/jit(cholesky)/cholesky | solution.py:19
  198.0 0.6 compare_reduce_fusion.1
  198.7 0.7 fusion.33
  199.3 9.8 %custom-call.6 = f32[1,128,128]{1,2,0:T(8,128)S(1)} custom-call(f32[1,128,128]{2,1,0:T(8,128)S(1)} %fusion.33), custom_call_target="InvertDiagBlocksLowerTriangular" | custom-call | tf_op jit(solution)/shard_map/triangular_solve/custom-call.0 | solution.py:20
  209.2 0.4 fusion.11
  209.6 0.6 gather_fusion.2
  210.2 0.7 broadcast_select_fusion.2
  210.9 4.5 %all-to-all-start.5 = ((bf16[8,32,128]{2,1,0:T(8,128)(2,1)}), bf16[8,32,128]{2,1,0:T(8,128)(2,1)S(1)}, u32[]{:S(2)}, u32[]{:S(2)}) async-start(bf16[8,32,128]{2,1,0:T(8,128)(2,1)} %broadcast_select_fusion.2), calls=%async_computation.5 | async-start | bytes 131072 | tf_op jit(solution)/shard_map/all_to_all | solution.py:94
  215.4 0.9 fusion.21
  216.3 6.0 %all-to-all-done.5 = bf16[8,32,128]{2,1,0:T(8,128)(2,1)S(1)} async-done(((bf16[8,32,128]{2,1,0:T(8,128)(2,1)}), bf16[8,32,128]{2,1,0:T(8,128)(2,1)S(1)}, u32[]{:S(2)}, u32[]{:S(2)}) %all-to-all-start.5) | async-done | bytes 65568 | tf_op jit(solution)/shard_map/all_to_all | solution.py:94
  222.3 3.4 all-to-all-start.6
  225.7 0.2 all-reduce.9.cloned.1.call-start
  225.9 0.3 convolution_bitcast_fusion.1
  226.2 6.8 %all-to-all-done.6 = f32[8,32,128]{2,1,0:T(8,128)S(1)} async-done(((f32[8,32,128]{2,1,0:T(8,128)}), f32[8,32,128]{2,1,0:T(8,128)S(1)}, u32[]{:S(2)}, u32[]{:S(2)}) %all-to-all-start.6) | async-done | bytes 131104 | tf_op jit(solution)/shard_map/all_to_all | solution.py:93
  233.0 0.3 fusion.25
  233.3 0.1 bitcast_multiply_fusion
  233.4 0.9 fusion.4
  234.4 30.1 %all-reduce.9.cloned.1.call-done = f32[512,128]{1,0:T(8,128)} async-done(((f32[512,128]{1,0:T(8,128)}), f32[512,128]{1,0:T(8,128)}) %all-reduce.9.cloned.1.call-update) | async-done | bytes 262160 | tf_op jit(solution)/shard_map/psum | solution.py:106
  264.5 2.5 fusion.16
  267.0 70.0 %all-reduce.11.cloned.1.call-done = f32[128,128]{0,1:T(8,128)} async-done(((f32[128,128]{0,1:T(8,128)}), f32[128,128]{0,1:T(8,128)}) %all-reduce.11.cloned.1.call-update) | async-done | bytes 65552 | tf_op jit(solution)/shard_map/psum | solution.py:108
  337.0 0.9 copy.35
  338.0 0.9 fusion.36
  338.8 11.7 %cholesky.55 = f32[128,128]{1,0:T(8,128)S(1)} custom-call(f32[128,128]{1,0:T(8,128)S(1)} %fusion.36), custom_call_target="Cholesky" | custom-call | tf_op jit(solution)/shard_map/jit(cholesky)/cholesky | solution.py:19
  350.6 0.6 compare_reduce_fusion
  351.2 0.7 fusion.34
  351.9 9.8 %custom-call.7 = f32[1,128,128]{1,2,0:T(8,128)S(1)} custom-call(f32[1,128,128]{2,1,0:T(8,128)S(1)} %fusion.34), custom_call_target="InvertDiagBlocksLowerTriangular" | custom-call | tf_op jit(solution)/shard_map/triangular_solve/custom-call.0 | solution.py:20
  361.7 0.5 fusion.6
  362.2 0.8 copy.36
  (40 shorter events, 0.6 us)
Async XLA Ops:
  6.5 10.3 %copy-start = (bf16[512,1024]{1,0:T(8,128)(2,1)S(1)}, bf16[512,1024]{1,0:T(8,128)(2,1)}, u32[]{:S(2)}) copy-start(bf16[512,1024]{1,0:T(8,128)(2,1)} %param.8) | copy-start | bytes 3145732
  7.9 13.7 %all-to-all-start = ((s32[8,1,1]{2,1,0:T(1,128)}), s32[8,1,1]{2,1,0:T(1,128)S(1)}, u32[]{:S(2)}, u32[]{:S(2)}) async-start(s32[8,1,1]{2,1,0:T(1,128)} %copy.25), calls=%async_computation | async-start | bytes 8192 | tf_op jit(solution)/shard_map/all_to_all | solution.py:53
  22.7 4.4 %copy-start.4 = (s32[1,8]{1,0:T(1,128)S(1)}, s32[1,8]{1,0:T(1,128)}, u32[]{:S(2)}) copy-start(s32[1,8]{1,0:T(1,128)} %param.10) | copy-start | bytes 100
  23.6 16.8 %all-to-all-start.1 = ((bf16[8,32,1024]{2,1,0:T(8,128)(2,1)}), bf16[8,32,1024]{2,1,0:T(8,128)(2,1)S(1)}, u32[]{:S(2)}, u32[]{:S(2)}) async-start(bf16[8,32,1024]{2,1,0:T(8,128)(2,1)} %broadcast_select_fusion), calls=%async_computation.1 | async-start | bytes 1048576 | tf_op jit(solution)/shard_map/all_to_all | solution.py:59
  40.5 17.2 %copy-start.3 = (bf16[512,128]{1,0:T(8,128)(2,1)S(1)}, bf16[512,128]{1,0:T(8,128)(2,1)}, u32[]{:S(2)}) copy-start(bf16[512,128]{1,0:T(8,128)(2,1)} %param.9) | copy-start | bytes 393220
  41.8 10.1 %all-to-all-start.2 = ((f32[8,1,32]{2,1,0:T(1,128)}), f32[8,1,32]{2,1,0:T(1,128)S(1)}, u32[]{:S(2)}, u32[]{:S(2)}) async-start(f32[8,1,32]{2,1,0:T(1,128)} %bitcast.6), calls=%async_computation.2 | async-start | bytes 8192 | tf_op jit(solution)/shard_map/all_to_all | solution.py:83
  59.2 10.2 %all-to-all-start.3 = ((bf16[8,32,128]{2,1,0:T(8,128)(2,1)}), bf16[8,32,128]{2,1,0:T(8,128)(2,1)S(1)}, u32[]{:S(2)}, u32[]{:S(2)}) async-start(bf16[8,32,128]{2,1,0:T(8,128)(2,1)} %broadcast_select_fusion.1), calls=%async_computation.3 | async-start | bytes 131072 | tf_op jit(solution)/shard_map/all_to_all | solution.py:94
  69.4 10.7 %all-to-all-start.4 = ((f32[8,32,128]{2,1,0:T(8,128)}), f32[8,32,128]{2,1,0:T(8,128)S(1)}, u32[]{:S(2)}, u32[]{:S(2)}) async-start(f32[8,32,128]{2,1,0:T(8,128)} %fusion.23), calls=%async_computation.4 | async-start | bytes 262144 | tf_op jit(solution)/shard_map/all_to_all | solution.py:93
  72.7 39.1 %all-reduce.5.cloned.1.call-start = ((), (), s32[]{:S(2)}) async-start(), calls=%async_computation.7 | async-start | bytes 524288 | tf_op jit(solution)/shard_map/psum | solution.py:106
  81.4 103.1 %all-reduce.7.cloned.1.call-start = ((), (), s32[]{:S(2)}) async-start(), calls=%async_computation.8 | async-start | bytes 131072 | tf_op jit(solution)/shard_map/psum | solution.py:108
  111.8 97.3 %copy-start.1 = (f32[512,128]{1,0:T(8,128)S(1)}, f32[512,128]{1,0:T(8,128)}, u32[]{:S(2)}) copy-start(f32[512,128]{1,0:T(8,128)} %all-reduce.5.cloned.1.call-done) | copy-start | bytes 786436
  210.9 11.4 %all-to-all-start.5 = ((bf16[8,32,128]{2,1,0:T(8,128)(2,1)}), bf16[8,32,128]{2,1,0:T(8,128)(2,1)S(1)}, u32[]{:S(2)}, u32[]{:S(2)}) async-start(bf16[8,32,128]{2,1,0:T(8,128)(2,1)} %broadcast_select_fusion.2), calls=%async_computation.5 | async-start | bytes 131072 | tf_op jit(solution)/shard_map/all_to_all | solution.py:94
  222.3 10.7 %all-to-all-start.6 = ((f32[8,32,128]{2,1,0:T(8,128)}), f32[8,32,128]{2,1,0:T(8,128)S(1)}, u32[]{:S(2)}, u32[]{:S(2)}) async-start(f32[8,32,128]{2,1,0:T(8,128)} %fusion.21), calls=%async_computation.6 | async-start | bytes 262144 | tf_op jit(solution)/shard_map/all_to_all | solution.py:93
  225.7 38.8 %all-reduce.9.cloned.1.call-start = ((), (), s32[]{:S(2)}) async-start(), calls=%async_computation.9 | async-start | bytes 524288 | tf_op jit(solution)/shard_map/psum | solution.py:106
  234.3 102.7 %all-reduce.11.cloned.1.call-start = ((), (), s32[]{:S(2)}) async-start(), calls=%async_computation.10 | async-start | bytes 131072 | tf_op jit(solution)/shard_map/psum | solution.py:108
  264.5 97.2 %copy-start.2 = (f32[512,128]{1,0:T(8,128)S(1)}, f32[512,128]{1,0:T(8,128)}, u32[]{:S(2)}) copy-start(f32[512,128]{1,0:T(8,128)} %all-reduce.9.cloned.1.call-done) | copy-start | bytes 786436
Sparse Core Ops, SparseCore 0:
  81.5 30.2 all-reduce.4
  115.2 69.2 all-reduce.6
  234.5 29.9 all-reduce.8
  267.8 69.2 all-reduce.10
where the time goes:
time: 371 us; the launch traced here: 370 us
  waiting for transfers between devices  250 us (67%)
  other arithmetic  52.4 us (14%)
  starting transfers between devices  29.4 us (8%)
  between operations  13.5 us (4%)
  matrix products  12.4 us (3%)
  local copies, waits for them, and re-layouts  6.14 us (2%)
  blocking collectives  5.65 us (2%)
    psum x2, waiting for transfers between devices, on_device(): gram_matrix = lax.psum(jnp.dot(result.T, result, precision=highest), 'rows')  140 us
    psum x2, waiting for transfers between devices, on_device(): summed_all = lax.psum(summed_part, 'rep')  60.5 us
    another operation x6, other arithmetic, orthonormal(): lower_factor = jnp.linalg.cholesky(gram_matrix)  24.8 us
    another operation x4, other arithmetic, orthonormal(): lax.linalg.triangular_solve(lower_factor, result, left_side=False, lower=...  20.9 us
    all_to_all x2, waiting for transfers between devices, on_device(): lax.all_to_all(reverse, 'rows', split_axis=0, concat_axis=0, tiled=True)  13.7 us
    all_to_all x1, waiting for transfers between devices, on_device(): lax.all_to_all(outgoing, 'rows', split_axis=0, concat_axis=0, tiled=True)  12.7 us
    all_to_all x2, waiting for transfers between devices, on_device(): lax.all_to_all(outgoing_iterate, 'rows', split_axis=0, concat_axis=0, til...  12 us
    all_to_all x2, starting transfers between devices, on_device(): lax.all_to_all(outgoing_iterate, 'rows', split_axis=0, concat_axis=0, til...  7.89 us
  transfers between devices with their start and end apart: 11, of which 11 were waited for; matrix products, arithmetic and copies ran while one was open for 1% of the time, Pallas kernels for 0%

commit v1 on v0

--- a/solution.py
+++ b/solution.py
@@ -105,7 +105,9 @@
         summed_part = forward + widen(placed, rep_count, quarter_index)
         summed_all = lax.psum(summed_part, "rep")
         result = summed_all * inv_root[:, None]
-        gram_matrix = lax.psum(jnp.dot(result.T, result, precision=highest), "rows")
+        gram_matrix = jnp.sum(
+            lax.all_gather(jnp.dot(result.T, result, precision=highest), "rows"), axis=0
+        )
         current = orthonormal(result, gram_matrix)
         scaled = (current * inv_root[:, None]).astype(jnp.bfloat16)
     return current * math.sqrt(slab_rows * rows_count)

time: 371 us -> 289 us (0.78)
  waiting for transfers between devices: 250 us -> 109 us
  blocking collectives: 5.65 us -> 68.9 us
    psum x2 -> x0, waiting for transfers between devices: 140 us -> none  [on_device(): gram_matrix = lax.psum(jnp.dot(result.T, result, precision=highest), 'rows')]
    all_gather x0 -> x2, blocking collectives: none -> 63.2 us  [on_device(): lax.all_gather(jnp.dot(result.T, result, precision=highest), 'rows')]
  transfers between devices with their start and end apart: 11 -> 9, of which waited for: 11 -> 9; matrix products, arithmetic and copies ran while one was open for 1% -> 2% of each run, Pallas kernels for 0% -> 0%
where the time goes in v1:
time: 289 us; the launch traced here: 288 us
  waiting for transfers between devices  109 us (38%)
  blocking collectives  68.9 us (24%)
  other arithmetic  50.8 us (18%)
  starting transfers between devices  30.1 us (10%)
  between operations  13.8 us (5%)
  matrix products  11.1 us (4%)
  local copies, waits for them, and re-layouts  4.47 us (2%)
    all_gather x2, blocking collectives, on_device(): lax.all_gather(jnp.dot(result.T, result, precision=highest), 'rows')  63.2 us
    psum x2, waiting for transfers between devices, on_device(): summed_all = lax.psum(summed_part, 'rep')  59.7 us
    another operation x6, other arithmetic, orthonormal(): lower_factor = jnp.linalg.cholesky(gram_matrix)  24.8 us
    another operation x4, other arithmetic, orthonormal(): lax.linalg.triangular_solve(lower_factor, result, left_side=False, lower=...  20.9 us
    all_to_all x2, waiting for transfers between devices, on_device(): lax.all_to_all(reverse, 'rows', split_axis=0, concat_axis=0, tiled=True)  13.7 us
    all_to_all x1, waiting for transfers between devices, on_device(): lax.all_to_all(outgoing, 'rows', split_axis=0, concat_axis=0, tiled=True)  12.7 us
    all_to_all x2, waiting for transfers between devices, on_device(): lax.all_to_all(outgoing_iterate, 'rows', split_axis=0, concat_axis=0, til...  12 us
    all_to_all x2, starting transfers between devices, on_device(): lax.all_to_all(outgoing_iterate, 'rows', split_axis=0, concat_axis=0, til...  8.64 us
  transfers between devices with their start and end apart: 9, of which 9 were waited for; matrix products, arithmetic and copies ran while one was open for 2% of the time, Pallas kernels for 0%

profile of v1, /device:TPU:0, one launch (start us, length us, event | category | flops | bytes accessed | tf_op | source)
XLA Modules:
  0.0 288.2 jit_solution(2613524726807674382)
XLA Ops:
  6.5 1.4 copy.21
  7.9 7.3 %all-to-all-start = ((s32[8,1,1]{2,1,0:T(1,128)}), s32[8,1,1]{2,1,0:T(1,128)S(1)}, u32[]{:S(2)}, u32[]{:S(2)}) async-start(s32[8,1,1]{2,1,0:T(1,128)} %copy.21), calls=%async_computation | async-start | bytes 8192 | tf_op jit(solution)/shard_map/all_to_all | solution.py:53
  15.3 0.1 iota_add_fusion
  15.3 1.5 multiply_reduce_fusion
  16.9 0.1 multiply_reduce_fusion.2
  17.0 0.1 mul.173
  17.1 0.1 mul.174
  17.2 4.5 %all-to-all-done = s32[8,1,1]{2,1,0:T(1,128)S(1)} async-done(((s32[8,1,1]{2,1,0:T(1,128)}), s32[8,1,1]{2,1,0:T(1,128)S(1)}, u32[]{:S(2)}, u32[]{:S(2)}) %all-to-all-start) | async-done | bytes 64 | tf_op jit(solution)/shard_map/all_to_all | solution.py:53
  21.7 0.4 fusion.50
  22.1 0.6 gather_fusion
  22.7 0.9 broadcast_select_fusion
  23.6 3.5 %all-to-all-start.1 = ((bf16[8,32,1024]{2,1,0:T(8,128)(2,1)}), bf16[8,32,1024]{2,1,0:T(8,128)(2,1)S(1)}, u32[]{:S(2)}, u32[]{:S(2)}) async-start(bf16[8,32,1024]{2,1,0:T(8,128)(2,1)} %broadcast_select_fusion), calls=%async_computation.1 | async-start | bytes 1048576 | tf_op jit(solution)/shard_map/all_to_all | solution.py:59
  27.1 0.5 convert_reduce_fusion.2
  27.7 12.7 %all-to-all-done.1 = bf16[8,32,1024]{2,1,0:T(8,128)(2,1)S(1)} async-done(((bf16[8,32,1024]{2,1,0:T(8,128)(2,1)}), bf16[8,32,1024]{2,1,0:T(8,128)(2,1)S(1)}, u32[]{:S(2)}, u32[]{:S(2)}) %all-to-all-start.1) | async-done | bytes 524320 | tf_op jit(solution)/shard_map/all_to_all | solution.py:59
  40.4 0.2 multiply_reduce_fusion.1
  40.6 1.2 convert_reduce_fusion.1
  41.8 3.7 %all-to-all-start.2 = ((f32[8,1,32]{2,1,0:T(1,128)}), f32[8,1,32]{2,1,0:T(1,128)S(1)}, u32[]{:S(2)}, u32[]{:S(2)}) async-start(f32[8,1,32]{2,1,0:T(1,128)} %bitcast.6), calls=%async_computation.2 | async-start | bytes 8192 | tf_op jit(solution)/shard_map/all_to_all | solution.py:83
  45.4 6.4 %all-to-all-done.2 = f32[8,1,32]{2,1,0:T(1,128)S(1)} async-done(((f32[8,1,32]{2,1,0:T(1,128)}), f32[8,1,32]{2,1,0:T(1,128)S(1)}, u32[]{:S(2)}, u32[]{:S(2)}) %all-to-all-start.2) | async-done | bytes 1056 | tf_op jit(solution)/shard_map/all_to_all | solution.py:83
  51.9 0.1 fusion.42
  52.0 0.1 mul.172
  52.1 5.7 %psum.21 = f32[512]{0:T(512)S(1)} all-reduce(f32[512]{0:T(512)S(1)} %multiply_add_fusion), channel_id=1, replica_groups=mesh['rows'=8,'rep'=4] {'rep'}, use_global_device_ids=true, to_apply=%region_6.7 | all-reduce | flops 512 | bytes 4096 | tf_op jit(solution)/shard_map/psum | solution.py:85
  57.7 0.1 multiply_convert_fusion
  57.9 0.6 gather_fusion.1
  58.5 0.7 broadcast_select_fusion.1
  59.2 3.3 %all-to-all-start.3 = ((bf16[8,32,128]{2,1,0:T(8,128)(2,1)}), bf16[8,32,128]{2,1,0:T(8,128)(2,1)S(1)}, u32[]{:S(2)}, u32[]{:S(2)}) async-start(bf16[8,32,128]{2,1,0:T(8,128)(2,1)} %broadcast_select_fusion.1), calls=%async_computation.3 | async-start | bytes 131072 | tf_op jit(solution)/shard_map/all_to_all | solution.py:94
  62.5 0.9 fusion.23
  63.4 6.0 %all-to-all-done.3 = bf16[8,32,128]{2,1,0:T(8,128)(2,1)S(1)} async-done(((bf16[8,32,128]{2,1,0:T(8,128)(2,1)}), bf16[8,32,128]{2,1,0:T(8,128)(2,1)S(1)}, u32[]{:S(2)}, u32[]{:S(2)}) %all-to-all-start.3) | async-done | bytes 65568 | tf_op jit(solution)/shard_map/all_to_all | solution.py:94
  69.4 3.4 %all-to-all-start.4 = ((f32[8,32,128]{2,1,0:T(8,128)}), f32[8,32,128]{2,1,0:T(8,128)S(1)}, u32[]{:S(2)}, u32[]{:S(2)}) async-start(f32[8,32,128]{2,1,0:T(8,128)} %fusion.23), calls=%async_computation.4 | async-start | bytes 262144 | tf_op jit(solution)/shard_map/all_to_all | solution.py:93
  72.8 0.3 convolution_bitcast_fusion.3
  73.1 6.9 %all-to-all-done.4 = f32[8,32,128]{2,1,0:T(8,128)S(1)} async-done(((f32[8,32,128]{2,1,0:T(8,128)}), f32[8,32,128]{2,1,0:T(8,128)S(1)}, u32[]{:S(2)}, u32[]{:S(2)}) %all-to-all-start.4) | async-done | bytes 131104 | tf_op jit(solution)/shard_map/all_to_all | solution.py:93
  80.0 0.3 fusion.27
  80.3 0.1 bitcast_multiply_fusion.1
  80.4 0.9 fusion.5
  81.4 30.4 %all-reduce.3.cloned.1.call-done = f32[512,128]{1,0:T(8,128)} async-done(((f32[512,128]{1,0:T(8,128)}), f32[512,128]{1,0:T(8,128)}) %all-reduce.3.cloned.1.call-update) | async-done | bytes 262160 | tf_op jit(solution)/shard_map/psum | solution.py:106
  111.8 1.9 fusion.19
  113.7 31.6 %all-gather = f32[1024,128]{1,0:T(8,128)S(1)} all-gather(f32[128,128]{1,0:T(8,128)S(1)} %fusion.19), channel_id=2, replica_groups=mesh['rows'=8,'rep'=4] {'rows'}, dimensions={0}, use_global_device_ids=true | all-gather | bytes 589824 | tf_op jit(solution)/shard_map/all_gather | solution.py:109
  145.3 0.1 copy.25
  145.4 11.7 %cholesky.44 = f32[128,128]{1,0:T(8,128)S(1)} custom-call(f32[128,128]{1,0:T(8,128)S(1)} %fusion.38), custom_call_target="Cholesky" | custom-call | tf_op jit(solution)/shard_map/jit(cholesky)/cholesky | solution.py:19
  157.2 0.6 compare_reduce_fusion.1
  157.8 0.7 fusion.33
  158.5 9.8 %custom-call.6 = f32[1,128,128]{1,2,0:T(8,128)S(1)} custom-call(f32[1,128,128]{2,1,0:T(8,128)S(1)} %fusion.33), custom_call_target="InvertDiagBlocksLowerTriangular" | custom-call | tf_op jit(solution)/shard_map/triangular_solve/custom-call.0 | solution.py:20
  168.3 0.4 fusion.11
  168.7 0.6 gather_fusion.2
  169.3 0.7 broadcast_select_fusion.2
  170.0 5.3 %all-to-all-start.5 = ((bf16[8,32,128]{2,1,0:T(8,128)(2,1)}), bf16[8,32,128]{2,1,0:T(8,128)(2,1)S(1)}, u32[]{:S(2)}, u32[]{:S(2)}) async-start(bf16[8,32,128]{2,1,0:T(8,128)(2,1)} %broadcast_select_fusion.2), calls=%async_computation.5 | async-start | bytes 131072 | tf_op jit(solution)/shard_map/all_to_all | solution.py:94
  175.3 0.9 fusion.21
  176.2 6.0 %all-to-all-done.5 = bf16[8,32,128]{2,1,0:T(8,128)(2,1)S(1)} async-done(((bf16[8,32,128]{2,1,0:T(8,128)(2,1)}), bf16[8,32,128]{2,1,0:T(8,128)(2,1)S(1)}, u32[]{:S(2)}, u32[]{:S(2)}) %all-to-all-start.5) | async-done | bytes 65568 | tf_op jit(solution)/shard_map/all_to_all | solution.py:94
  182.2 3.4 %all-to-all-start.6 = ((f32[8,32,128]{2,1,0:T(8,128)}), f32[8,32,128]{2,1,0:T(8,128)S(1)}, u32[]{:S(2)}, u32[]{:S(2)}) async-start(f32[8,32,128]{2,1,0:T(8,128)} %fusion.21), calls=%async_computation.6 | async-start | bytes 262144 | tf_op jit(solution)/shard_map/all_to_all | solution.py:93
  185.6 0.2 all-reduce.5.cloned.1.call-start
  185.8 0.3 convolution_bitcast_fusion.1
  186.1 6.8 %all-to-all-done.6 = f32[8,32,128]{2,1,0:T(8,128)S(1)} async-done(((f32[8,32,128]{2,1,0:T(8,128)}), f32[8,32,128]{2,1,0:T(8,128)S(1)}, u32[]{:S(2)}, u32[]{:S(2)}) %all-to-all-start.6) | async-done | bytes 131104 | tf_op jit(solution)/shard_map/all_to_all | solution.py:93
  192.9 0.3 fusion.25
  193.1 0.1 bitcast_multiply_fusion
  193.3 0.9 fusion.4
  194.2 29.3 %all-reduce.5.cloned.1.call-done = f32[512,128]{1,0:T(8,128)} async-done(((f32[512,128]{1,0:T(8,128)}), f32[512,128]{1,0:T(8,128)}) %all-reduce.5.cloned.1.call-update) | async-done | bytes 262160 | tf_op jit(solution)/shard_map/psum | solution.py:106
  223.5 1.9 fusion.16
  225.3 31.6 %all-gather.1 = f32[1024,128]{1,0:T(8,128)S(1)} all-gather(f32[128,128]{1,0:T(8,128)S(1)} %fusion.16), channel_id=3, replica_groups=mesh['rows'=8,'rep'=4] {'rows'}, dimensions={0}, use_global_device_ids=true | all-gather | bytes 589824 | tf_op jit(solution)/shard_map/all_gather | solution.py:109
  257.0 0.1 copy.29
  257.1 11.7 %cholesky.55 = f32[128,128]{1,0:T(8,128)S(1)} custom-call(f32[128,128]{1,0:T(8,128)S(1)} %fusion.36), custom_call_target="Cholesky" | custom-call | tf_op jit(solution)/shard_map/jit(cholesky)/cholesky | solution.py:19
  268.8 0.6 compare_reduce_fusion
  269.5 0.7 fusion.34
  270.2 9.8 %custom-call.7 = f32[1,128,128]{1,2,0:T(8,128)S(1)} custom-call(f32[1,128,128]{2,1,0:T(8,128)S(1)} %fusion.34), custom_call_target="InvertDiagBlocksLowerTriangular" | custom-call | tf_op jit(solution)/shard_map/triangular_solve/custom-call.0 | solution.py:20
  280.0 0.5 fusion.6
  280.5 0.8 copy.30
  (38 shorter events, 0.4 us)
Async XLA Ops:
  6.5 10.3 %copy-start = (bf16[512,1024]{1,0:T(8,128)(2,1)S(1)}, bf16[512,1024]{1,0:T(8,128)(2,1)}, u32[]{:S(2)}) copy-start(bf16[512,1024]{1,0:T(8,128)(2,1)} %param.8) | copy-start | bytes 3145732
  7.9 13.7 %all-to-all-start = ((s32[8,1,1]{2,1,0:T(1,128)}), s32[8,1,1]{2,1,0:T(1,128)S(1)}, u32[]{:S(2)}, u32[]{:S(2)}) async-start(s32[8,1,1]{2,1,0:T(1,128)} %copy.21), calls=%async_computation | async-start | bytes 8192 | tf_op jit(solution)/shard_map/all_to_all | solution.py:53
  22.7 4.4 %copy-start.4 = (s32[1,8]{1,0:T(1,128)S(1)}, s32[1,8]{1,0:T(1,128)}, u32[]{:S(2)}) copy-start(s32[1,8]{1,0:T(1,128)} %param.10) | copy-start | bytes 100
  23.6 16.8 %all-to-all-start.1 = ((bf16[8,32,1024]{2,1,0:T(8,128)(2,1)}), bf16[8,32,1024]{2,1,0:T(8,128)(2,1)S(1)}, u32[]{:S(2)}, u32[]{:S(2)}) async-start(bf16[8,32,1024]{2,1,0:T(8,128)(2,1)} %broadcast_select_fusion), calls=%async_computation.1 | async-start | bytes 1048576 | tf_op jit(solution)/shard_map/all_to_all | solution.py:59
  40.5 17.2 %copy-start.3 = (bf16[512,128]{1,0:T(8,128)(2,1)S(1)}, bf16[512,128]{1,0:T(8,128)(2,1)}, u32[]{:S(2)}) copy-start(bf16[512,128]{1,0:T(8,128)(2,1)} %param.9) | copy-start | bytes 393220
  41.8 10.1 %all-to-all-start.2 = ((f32[8,1,32]{2,1,0:T(1,128)}), f32[8,1,32]{2,1,0:T(1,128)S(1)}, u32[]{:S(2)}, u32[]{:S(2)}) async-start(f32[8,1,32]{2,1,0:T(1,128)} %bitcast.6), calls=%async_computation.2 | async-start | bytes 8192 | tf_op jit(solution)/shard_map/all_to_all | solution.py:83
  59.2 10.2 %all-to-all-start.3 = ((bf16[8,32,128]{2,1,0:T(8,128)(2,1)}), bf16[8,32,128]{2,1,0:T(8,128)(2,1)S(1)}, u32[]{:S(2)}, u32[]{:S(2)}) async-start(bf16[8,32,128]{2,1,0:T(8,128)(2,1)} %broadcast_select_fusion.1), calls=%async_computation.3 | async-start | bytes 131072 | tf_op jit(solution)/shard_map/all_to_all | solution.py:94
  69.4 10.7 %all-to-all-start.4 = ((f32[8,32,128]{2,1,0:T(8,128)}), f32[8,32,128]{2,1,0:T(8,128)S(1)}, u32[]{:S(2)}, u32[]{:S(2)}) async-start(f32[8,32,128]{2,1,0:T(8,128)} %fusion.23), calls=%async_computation.4 | async-start | bytes 262144 | tf_op jit(solution)/shard_map/all_to_all | solution.py:93
  72.7 39.1 %all-reduce.3.cloned.1.call-start = ((), (), s32[]{:S(2)}) async-start(), calls=%async_computation.7 | async-start | bytes 524288 | tf_op jit(solution)/shard_map/psum | solution.py:106
  111.8 56.5 %copy-start.1 = (f32[512,128]{1,0:T(8,128)S(1)}, f32[512,128]{1,0:T(8,128)}, u32[]{:S(2)}) copy-start(f32[512,128]{1,0:T(8,128)} %all-reduce.3.cloned.1.call-done) | copy-start | bytes 786436
  170.0 12.2 %all-to-all-start.5 = ((bf16[8,32,128]{2,1,0:T(8,128)(2,1)}), bf16[8,32,128]{2,1,0:T(8,128)(2,1)S(1)}, u32[]{:S(2)}, u32[]{:S(2)}) async-start(bf16[8,32,128]{2,1,0:T(8,128)(2,1)} %broadcast_select_fusion.2), calls=%async_computation.5 | async-start | bytes 131072 | tf_op jit(solution)/shard_map/all_to_all | solution.py:94
  182.2 10.7 %all-to-all-start.6 = ((f32[8,32,128]{2,1,0:T(8,128)}), f32[8,32,128]{2,1,0:T(8,128)S(1)}, u32[]{:S(2)}, u32[]{:S(2)}) async-start(f32[8,32,128]{2,1,0:T(8,128)} %fusion.21), calls=%async_computation.6 | async-start | bytes 262144 | tf_op jit(solution)/shard_map/all_to_all | solution.py:93
  185.6 37.9 %all-reduce.5.cloned.1.call-start = ((), (), s32[]{:S(2)}) async-start(), calls=%async_computation.8 | async-start | bytes 524288 | tf_op jit(solution)/shard_map/psum | solution.py:106
  223.5 56.5 %copy-start.2 = (f32[512,128]{1,0:T(8,128)S(1)}, f32[512,128]{1,0:T(8,128)}, u32[]{:S(2)}) copy-start(f32[512,128]{1,0:T(8,128)} %all-reduce.5.cloned.1.call-done) | copy-start | bytes 786436
Sparse Core Ops, SparseCore 0:
  81.5 30.2 all-reduce.2
  194.3 29.1 all-reduce.4
